TPU v7x, 512 devices: a whole 4x8x8 slice. The times are simulated.
512 devices in a mesh: pp: 16 (over z, core), ep: 32 (over x, y).
Axes of the slice: x: 4, y: 8, z: 8, core: 2. Of those that a mesh axis runs over, the one named last changes fastest.
Arguments:
- pending_activations: bfloat16 [16, 2048, 3584], P('pp', 'ep'), may hold values from -6 to 6
- incoming_microbatches: bfloat16 [1, 2048, 3584], P(None, 'ep'), may hold values from -6 to 6
- layer_rescale_factor: float32 [16, 3584], P('pp'), may hold values from 0.5 to 1.5
- gating_projection_matrix: bfloat16 [16, 3584, 4096], P('pp', None, 'ep'), may hold values from -0.09375 to 0.09375
- widening_projection_matrix: bfloat16 [16, 3584, 4096], P('pp', None, 'ep'), may hold values from -0.09375 to 0.09375
- output_projection_matrix: bfloat16 [16, 4096, 3584], P('pp', 'ep'), may hold values from -0.1875 to 0.1875
- picked_specialist_ids: int32 [2, 16, 2048, 1], P(None, 'pp', 'ep'), may hold values from 0 to 3; in each aligned block of 64 rows (0 to 63, 64 to 127, ..., all dimensions but the last counted through in order) at most 17 rows name the same one
- dispatcher_probability_values: float32 [2, 16, 2048, 1], P(None, 'pp', 'ep'), may hold values from 0.1 to 1
Outputs:
- section_outputs: bfloat16 [2, 16, 2048, 3584], P(None, 'pp', 'ep')
Inputs may be any that keep to these rules, and one draw needn't show every extreme that they name: `picked_specialist_ids`: each token names exactly one expert. In each step and section, the 64 rows of one device (aligned blocks of the token dimension) name each expert at most 17 times, a bound that some block reaches.
All inputs are finite; a program needn't handle non-finite values.
Results may differ from a plain program's by a relative error of at most 0.0055.
Values may be sent and summed in bfloat16 or wider, within the bound.
No kernel may reach another device: no remote copies, remote signals or barrier semaphores. Data moves between devices by JAX's collectives and lax.ppermute only.
A program may use at most 64 MiB of HBM per device.

v0:
```python
import jax
import jax.numpy as jnp
from jax import lax
from jax.sharding import Mesh, PartitionSpec as P

GROUP = 8


def slots_of(chosen, slot_count, experts):
    hits = (chosen[:, None] == jnp.arange(experts, dtype=jnp.int32)[None, :]).astype(jnp.int32)
    before = jnp.cumsum(hits, axis=0) - hits
    return chosen * slot_count + jnp.sum(before * hits, axis=1)


def section_layer(inputs, gain_row, gate_w, up_w, down_w, chosen, scores):
    row_count, width = inputs.shape
    experts = lax.axis_size("x")
    ring = lax.axis_size("y")
    slot_count = 17
    float_rows = inputs.astype(jnp.float32)
    variance = jnp.mean(float_rows * float_rows, axis=-1, keepdims=True)
    normed = (float_rows * lax.rsqrt(variance + 1e-06) * gain_row).astype(jnp.bfloat16)
    slot_ids = slots_of(chosen[:, 0], slot_count, experts)
    slot_grid = jnp.arange(experts * slot_count, dtype=jnp.int32)
    picker = (slot_grid[:, None] == slot_ids[None, :]).astype(jnp.bfloat16)
    packed = jnp.dot(picker, normed, preferred_element_type=jnp.float32).astype(jnp.bfloat16)
    sent = packed.reshape(experts, slot_count, width)
    mine = lax.all_to_all(sent, "x", split_axis=0, concat_axis=0, tiled=True)
    mine = mine.reshape(experts * slot_count, width)
    held = experts * slot_count
    padded = -(-held // 8) * 8
    mine = jnp.pad(mine, ((0, padded - held), (0, 0)))
    rows = lax.all_gather(mine, "y", axis=0, tiled=True)
    gate_val = jnp.dot(rows, gate_w, preferred_element_type=jnp.float32)
    up_val = jnp.dot(rows, up_w, preferred_element_type=jnp.float32)
    active = (jax.nn.silu(gate_val) * up_val).astype(jnp.bfloat16)
    partial = jnp.dot(active, down_w, preferred_element_type=jnp.float32).astype(jnp.bfloat16)
    summed = lax.psum_scatter(partial, "y", scatter_dimension=0, tiled=True)
    back = summed[:held].reshape(experts, slot_count, width)
    back = lax.all_to_all(back, "x", split_axis=0, concat_axis=0, tiled=True)
    back = back.reshape(held, width)
    unpick = (slot_ids[:, None] == slot_grid[None, :]).astype(jnp.bfloat16)
    combined = scores * jnp.dot(unpick, back, preferred_element_type=jnp.float32)
    return (float_rows + combined).astype(jnp.bfloat16)


def local(pending, incoming, gain, gate_w, up_w, down_w, chosen, scores):
    tick_total = chosen.shape[0]
    first_section = lax.axis_index("pp") == 0
    count = lax.axis_size("pp")
    rows = pending[0]
    outputs = []
    for tick in range(tick_total):
        produced = section_layer(
            rows, gain[0], gate_w[0], up_w[0], down_w[0], chosen[tick, 0], scores[tick, 0]
        )
        outputs.append(produced)
        if tick + 1 < tick_total:
            passed = lax.ppermute(produced, "pp", [(i, i + 1) for i in range(count - 1)])
            rows = jnp.where(first_section, incoming[tick], passed)
    return jnp.stack(outputs)[:, None]


def solution(mesh):
    fine = Mesh(mesh.devices.reshape(mesh.shape["pp"], -1, GROUP), ("pp", "x", "y"))
    ep = ("x", "y")
    in_specs = (
        P("pp", ep, None),
        P(None, ep, None),
        P("pp", None),
        P("pp", None, ep),
        P("pp", None, ep),
        P("pp", ep, None),
        P(None, "pp", ep, None),
        P(None, "pp", ep, None),
    )
    out_specs = P(None, "pp", ep, None)
    return jax.shard_map(local, mesh=fine, in_specs=in_specs, out_specs=out_specs, check_vma=False)
```

profile of v0, /device:TPU:24, one launch (start us, length us, event | category | flops | bytes accessed | tf_op | source)
XLA Modules:
  0.0 347.5 jit_solution(16498930131038805519)
XLA Ops:
  6.5 1.3 fusion.10
  10.5 1.4 convolution_convert_fusion.3
  12.0 15.3 %all_to_all.20 = bf16[4,17,3584]{2,1,0:T(8,128)(2,1)S(1)} all-to-all(bf16[4,17,3584]{2,1,0:T(8,128)(2,1)S(1)} %reshape.78), channel_id=1, replica_groups=mesh['pp'=16,'x'=4,'y'=8] {'x'}, dimensions={0} | all-to-all | bytes 974848 | tf_op jit(solution)/shard_map/all_to_all | solution.py:28
  27.5 0.8 pad.7
  28.4 58.9 %all-gather.3.cloned.1.call-done = bf16[576,3584]{1,0:T(8,128)(2,1)} async-done(((bf16[72,3584]{1,0:T(8,128)(2,1)}), bf16[576,3584]{1,0:T(8,128)(2,1)}) %all-gather.3.cloned.1.call-update) | async-done | bytes 4128784 | tf_op jit(solution)/shard_map/all_gather | solution.py:33
  87.4 3.6 %fusion.21 = f32[576,128]{1,0:T(8,128)S(1)} fusion(bf16[576,3584]{1,0:T(8,128)(2,1)} %all-gather.3.cloned.1.call-done, bf16[1,3584,128]{2,1,0:T(8,128)(2,1)} %param.11), kind=kOutput, calls=%fused_computation.32 | convolution fusion | flops 528482304 | bytes 5341184 | tf_op jit(solution)/shard_map/dot_general | solution.py:34
  91.0 8.5 %convolution_convert_fusion.1 = bf16[576,3584]{1,0:T(8,128)(2,1)} fusion(bf16[576,3584]{1,0:T(8,128)(2,1)} %all-gather.3.cloned.1.call-done, bf16[1,128,3584]{2,1,0:T(8,128)(2,1)S(1)} %copy-done, bf16[1,3584,128]{2,1,0:T(8,128)(2,1)S(1)} %copy-done.2, f32[576,128]{1,0:T(8,128)S(1)} %fusion.21), kind=kOutput, calls=%fused_computation.1 | convolution fusion | flops 1059471360 | bytes 10387456 | tf_op jit(solution)/shard_map/dot_general | solution.py:37
  99.5 56.3 %reduce-scatter.3.cloned.1.call-done = bf16[72,3584]{1,0:T(8,128)(2,1)} async-done(((bf16[576,3584]{1,0:T(8,128)(2,1)}), bf16[72,3584]{1,0:T(8,128)(2,1)}) %reduce-scatter.3.cloned.1.call-update) | async-done | bytes 516112 | tf_op jit(solution)/shard_map/reduce_scatter | solution.py:38
  155.8 2.0 reshape.80
  157.9 4.2 %all-to-all-start.1 = ((bf16[4,17,3584]{2,1,0:T(8,128)(2,1)}), bf16[4,17,3584]{2,1,0:T(8,128)(2,1)S(1)}, u32[]{:S(2)}, u32[]{:S(2)}) async-start(bf16[4,17,3584]{2,1,0:T(8,128)(2,1)} %reshape.80), calls=%async_computation.2 | async-start | bytes 1376256 | tf_op jit(solution)/shard_map/all_to_all | solution.py:40
  162.1 11.1 %all-to-all-done.1 = bf16[4,17,3584]{2,1,0:T(8,128)(2,1)S(1)} async-done(((bf16[4,17,3584]{2,1,0:T(8,128)(2,1)}), bf16[4,17,3584]{2,1,0:T(8,128)(2,1)S(1)}, u32[]{:S(2)}, u32[]{:S(2)}) %all-to-all-start.1) | async-done | bytes 487456 | tf_op jit(solution)/shard_map/all_to_all | solution.py:40
  173.8 1.3 collective-permute-start
  175.1 1.4 collective-permute-done
  176.5 1.3 fusion.7
  178.3 12.1 %all_to_all.21 = bf16[4,17,3584]{2,1,0:T(8,128)(2,1)} all-to-all(bf16[4,17,3584]{2,1,0:T(8,128)(2,1)S(1)} %reshape.82), channel_id=1, replica_groups=mesh['pp'=16,'x'=4,'y'=8] {'x'}, dimensions={0} | all-to-all | bytes 974848 | tf_op jit(solution)/shard_map/all_to_all | solution.py:28
  190.4 1.3 reshape.83
  191.7 0.8 pad.8
  192.6 62.1 %all-gather.5.cloned.1.call-done = bf16[576,3584]{1,0:T(8,128)(2,1)} async-done(((bf16[72,3584]{1,0:T(8,128)(2,1)}), bf16[576,3584]{1,0:T(8,128)(2,1)}) %all-gather.5.cloned.1.call-update) | async-done | bytes 4128784 | tf_op jit(solution)/shard_map/all_gather | solution.py:33
  254.6 3.6 %fusion.19 = f32[576,128]{1,0:T(8,128)S(1)} fusion(bf16[576,3584]{1,0:T(8,128)(2,1)} %all-gather.5.cloned.1.call-done, bf16[1,3584,128]{2,1,0:T(8,128)(2,1)} %param.11), kind=kOutput, calls=%fused_computation.30 | convolution fusion | flops 528482304 | bytes 5341184 | tf_op jit(solution)/shard_map/dot_general | solution.py:34
  258.3 8.5 %convolution_convert_fusion = bf16[576,3584]{1,0:T(8,128)(2,1)} fusion(bf16[576,3584]{1,0:T(8,128)(2,1)} %all-gather.5.cloned.1.call-done, bf16[1,128,3584]{2,1,0:T(8,128)(2,1)S(1)} %copy-done, bf16[1,3584,128]{2,1,0:T(8,128)(2,1)S(1)} %copy-done.2, f32[576,128]{1,0:T(8,128)S(1)} %fusion.19), kind=kOutput, calls=%fused_computation | convolution fusion | flops 1059471360 | bytes 10387456 | tf_op jit(solution)/shard_map/dot_general | solution.py:37
  266.8 56.3 %reduce-scatter.5.cloned.1.call-done = bf16[72,3584]{1,0:T(8,128)(2,1)} async-done(((bf16[576,3584]{1,0:T(8,128)(2,1)}), bf16[72,3584]{1,0:T(8,128)(2,1)}) %reduce-scatter.5.cloned.1.call-update) | async-done | bytes 516112 | tf_op jit(solution)/shard_map/reduce_scatter | solution.py:38
  323.1 1.2 reshape.84
  324.3 15.2 %all_to_all.22 = bf16[4,17,3584]{2,1,0:T(8,128)(2,1)S(1)} all-to-all(bf16[4,17,3584]{2,1,0:T(8,128)(2,1)S(1)} %reshape.84), channel_id=1, replica_groups=mesh['pp'=16,'x'=4,'y'=8] {'x'}, dimensions={0} | all-to-all | bytes 974848 | tf_op jit(solution)/shard_map/all_to_all | solution.py:40
  340.0 1.0 maximum_bitcast_fusion
  (39 shorter events, 4.7 us)
Async XLA Ops:
  6.5 84.5 %copy-start = (bf16[1,128,3584]{2,1,0:T(8,128)(2,1)S(1)}, bf16[1,128,3584]{2,1,0:T(8,128)(2,1)}, u32[]{:S(2)}) copy-start(bf16[1,128,3584]{2,1,0:T(8,128)(2,1)} %param.13) | copy-start | bytes 2752516
  6.5 80.8 %all-gather.3.cloned.1.call-start = ((), (), s32[]{:S(2)}) async-start(), calls=%async_computation.6 | async-start | bytes 4644864 | tf_op jit(solution)/shard_map/all_gather | solution.py:33
  27.5 63.5 %copy-start.2 = (bf16[1,3584,128]{2,1,0:T(8,128)(2,1)S(1)}, bf16[1,3584,128]{2,1,0:T(8,128)(2,1)}, u32[]{:S(2)}) copy-start(bf16[1,3584,128]{2,1,0:T(8,128)(2,1)} %param.12) | copy-start | bytes 2752516
  28.4 127.4 %reduce-scatter.3.cloned.1.call-start = ((), (), s32[]{:S(2)}) async-start(), calls=%async_computation.7 | async-start | bytes 4644864 | tf_op jit(solution)/shard_map/reduce_scatter | solution.py:38
  99.5 62.6 %copy-start.5 = (f32[2,1,64,1]{2,3,1,0:T(1,128)S(1)}, f32[2,1,64,1]{2,3,1,0:T(1,128)}, u32[]{:S(2)}) copy-start(f32[2,1,64,1]{2,3,1,0:T(1,128)} %param.15) | copy-start | bytes 1540
  99.5 73.9 %copy-start.1 = (bf16[1,64,3584]{2,1,0:T(8,128)(2,1)S(1)}, bf16[1,64,3584]{2,1,0:T(8,128)(2,1)}, u32[]{:S(2)}) copy-start(bf16[1,64,3584]{2,1,0:T(8,128)(2,1)} %param.8) | copy-start | bytes 1376260
  157.9 15.4 %all-to-all-start.1 = ((bf16[4,17,3584]{2,1,0:T(8,128)(2,1)}), bf16[4,17,3584]{2,1,0:T(8,128)(2,1)S(1)}, u32[]{:S(2)}, u32[]{:S(2)}) async-start(bf16[4,17,3584]{2,1,0:T(8,128)(2,1)} %reshape.80), calls=%async_computation.2 | async-start | bytes 1376256 | tf_op jit(solution)/shard_map/all_to_all | solution.py:40
  162.1 92.5 %all-gather.5.cloned.1.call-start = ((), (), s32[]{:S(2)}) async-start(), calls=%async_computation.8 | async-start | bytes 4644864 | tf_op jit(solution)/shard_map/all_gather | solution.py:33
  173.8 4.0 %copy-start.3 = (bf16[64,3584]{1,0:T(8,128)(2,1)}, bf16[64,3584]{1,0:T(8,128)(2,1)S(1)}, u32[]{:S(2)}) copy-start(bf16[64,3584]{1,0:T(8,128)(2,1)S(1)} %fusion.3) | copy-start | bytes 1376260
  173.8 2.7 collective-permute-start
  192.5 130.5 %reduce-scatter.5.cloned.1.call-start = ((), (), s32[]{:S(2)}) async-start(), calls=%async_computation.9 | async-start | bytes 4644864 | tf_op jit(solution)/shard_map/reduce_scatter | solution.py:38
  266.8 73.2 %copy-start.4 = (bf16[64,3584]{1,0:T(8,128)(2,1)S(1)}, bf16[64,3584]{1,0:T(8,128)(2,1)}, u32[]{:S(2)}) copy-start(bf16[64,3584]{1,0:T(8,128)(2,1)} %copy-done.3) | copy-start | bytes 1376260
Sparse Core Ops, SparseCore 0:
  28.5 58.7 all-gather.2
  99.7 56.0 reduce-scatter.2
  192.6 61.9 all-gather.4
  266.9 56.0 reduce-scatter.4
where the time goes:
time: 348 us
  waiting for transfers between devices  246 us (71%)
  blocking collectives  42.6 us (12%)
  matrix products  26.7 us (8%)
  between operations  13.3 us (4%)
  local copies, waits for them, and re-layouts  7.68 us (2%)
  starting transfers between devices  5.65 us (2%)
  other arithmetic  5.54 us (2%)
    all_gather x2, waiting for transfers between devices, section_layer(): rows = lax.all_gather(mine, 'y', axis=0, tiled=True)  121 us
    reduce_scatter x2, waiting for transfers between devices, section_layer(): summed = lax.psum_scatter(partial, 'y', scatter_dimension=0, tiled=True)  113 us
    all_to_all x2, blocking collectives, section_layer(): mine = lax.all_to_all(sent, 'x', split_axis=0, concat_axis=0, tiled=True)  27.4 us
    dot_general x2, matrix products, section_layer(): jnp.dot(active, down_w, preferred_element_type=jnp.float32)  17 us
    all_to_all x1, blocking collectives, section_layer(): back = lax.all_to_all(back, 'x', split_axis=0, concat_axis=0, tiled=True)  15.2 us
    all_to_all x1, waiting for transfers between devices, section_layer(): back = lax.all_to_all(back, 'x', split_axis=0, concat_axis=0, tiled=True)  11.1 us
    dot_general x2, matrix products, section_layer(): gate_val = jnp.dot(rows, gate_w, preferred_element_type=jnp.float32)  7.29 us
  transfers between devices with their start and end apart: 6, of which 6 were waited for; matrix products, arithmetic and copies ran while one was open for 0% of the time, Pallas kernels for 0%

commit v1 on v0

--- a/solution.py
+++ b/solution.py
@@ -30,7 +30,8 @@
     held = experts * slot_count
     padded = -(-held // 8) * 8
     mine = jnp.pad(mine, ((0, padded - held), (0, 0)))
-    rows = lax.all_gather(mine, "y", axis=0, tiled=True)
+    outgoing = jnp.stack([mine] * lax.axis_size("y"))
+    rows = jnp.concatenate(lax.all_to_all(outgoing, "y", 0, 0), axis=0)
     gate_val = jnp.dot(rows, gate_w, preferred_element_type=jnp.float32)
     up_val = jnp.dot(rows, up_w, preferred_element_type=jnp.float32)
     active = (jax.nn.silu(gate_val) * up_val).astype(jnp.bfloat16)

time: 348 us -> 427 us (1.23)
  blocking collectives: 42.6 us -> 234 us
  waiting for transfers between devices: 246 us -> 134 us
  matrix products: 26.7 us -> 21.8 us
    all_to_all x0 -> x2, blocking collectives: none -> 192 us  [section_layer(): rows = jnp.concatenate(lax.all_to_all(outgoing, 'y', 0, 0), axis=0)]
    all_gather x2 -> x0, waiting for transfers between devices: 121 us -> none  [section_layer(): rows = lax.all_gather(mine, 'y', axis=0, tiled=True)]
    reduce_scatter x2, waiting for transfers between devices: 113 us -> 122 us  [section_layer(): summed = lax.psum_scatter(partial, 'y', scatter_dimension=0, tiled=True)]
    dot_general x2, matrix products: 7.29 us -> 2.47 us  [section_layer(): gate_val = jnp.dot(rows, gate_w, preferred_element_type=jnp.float32)]
  transfers between devices with their start and end apart: 6 -> 4, of which waited for: 6 -> 4; matrix products, arithmetic and copies ran while one was open for 0% -> 0% of each run, Pallas kernels for 0% -> 0%
where the time goes in v1:
time: 427 us; the launch traced here: 426 us
  blocking collectives  234 us (55%)
  waiting for transfers between devices  134 us (31%)
  matrix products  21.8 us (5%)
  between operations  13.6 us (3%)
  local copies, waits for them, and re-layouts  10.5 us (2%)
  starting transfers between devices  5.56 us (1%)
  other arithmetic  5.54 us (1%)
    all_to_all x2, blocking collectives, section_layer(): rows = jnp.concatenate(lax.all_to_all(outgoing, 'y', 0, 0), axis=0)  192 us
    reduce_scatter x2, waiting for transfers between devices, section_layer(): summed = lax.psum_scatter(partial, 'y', scatter_dimension=0, tiled=True)  122 us
    all_to_all x2, blocking collectives, section_layer(): mine = lax.all_to_all(sent, 'x', split_axis=0, concat_axis=0, tiled=True)  27.4 us
    dot_general x2, matrix products, section_layer(): jnp.dot(active, down_w, preferred_element_type=jnp.float32)  17 us
    all_to_all x1, blocking collectives, section_layer(): back = lax.all_to_all(back, 'x', split_axis=0, concat_axis=0, tiled=True)  15.2 us
    all_to_all x1, waiting for transfers between devices, section_layer(): back = lax.all_to_all(back, 'x', split_axis=0, concat_axis=0, tiled=True)  11.2 us
  transfers between devices with their start and end apart: 4, of which 4 were waited for; matrix products, arithmetic and copies ran while one was open for 0% of the time, Pallas kernels for 0%

profile of v1, /device:TPU:24, one launch (start us, length us, event | category | flops | bytes accessed | tf_op | source)
XLA Modules:
  0.0 425.7 jit_solution(9548368392726385940)
XLA Ops:
  6.5 1.3 fusion.10
  10.5 1.4 convolution_convert_fusion.3
  12.0 15.3 %all_to_all.30 = bf16[4,17,3584]{2,1,0:T(8,128)(2,1)S(1)} all-to-all(bf16[4,17,3584]{2,1,0:T(8,128)(2,1)S(1)} %reshape.88), channel_id=1, replica_groups=mesh['pp'=16,'x'=4,'y'=8] {'x'}, dimensions={0} | all-to-all | bytes 974848 | tf_op jit(solution)/shard_map/all_to_all | solution.py:28
  27.9 97.1 %all_to_all.31 = bf16[8,72,3584]{2,1,0:T(8,128)(2,1)S(1)} all-to-all(bf16[8,72,3584]{2,1,0:T(8,128)(2,1)S(1)} %stack.10), channel_id=1, replica_groups=mesh['pp'=16,'x'=4,'y'=8] {'y'}, dimensions={0} | all-to-all | bytes 8257536 | tf_op jit(solution)/shard_map/all_to_all | solution.py:34
  125.0 1.9 copy-done.1
  126.9 1.2 fusion.21
  128.2 8.5 %convolution_convert_fusion.1 = bf16[576,3584]{1,0:T(8,128)(2,1)} fusion(bf16[576,3584]{1,0:T(8,128)(2,1)} %bitcast.58, bf16[1,128,3584]{2,1,0:T(8,128)(2,1)S(1)} %copy-done, bf16[1,3584,128]{2,1,0:T(8,128)(2,1)S(1)} %copy-done.4, f32[576,128]{1,0:T(8,128)S(1)} %fusion.21), kind=kOutput, calls=%fused_computation.1 | convolution fusion | flops 1059471360 | bytes 10387456 | tf_op jit(solution)/shard_map/dot_general | solution.py:38
  136.7 57.6 %reduce-scatter.3.cloned.1.call-done = bf16[72,3584]{1,0:T(8,128)(2,1)} async-done(((bf16[576,3584]{1,0:T(8,128)(2,1)}), bf16[72,3584]{1,0:T(8,128)(2,1)}) %reduce-scatter.3.cloned.1.call-update) | async-done | bytes 516112 | tf_op jit(solution)/shard_map/reduce_scatter | solution.py:39
  194.3 2.0 reshape.91
  196.4 4.2 all-to-all-start.2
  200.6 11.2 %all-to-all-done.2 = bf16[4,17,3584]{2,1,0:T(8,128)(2,1)S(1)} async-done(((bf16[4,17,3584]{2,1,0:T(8,128)(2,1)}), bf16[4,17,3584]{2,1,0:T(8,128)(2,1)S(1)}, u32[]{:S(2)}, u32[]{:S(2)}) %all-to-all-start.2) | async-done | bytes 487456 | tf_op jit(solution)/shard_map/all_to_all | solution.py:41
  212.4 1.3 collective-permute-start
  213.7 1.4 collective-permute-done
  215.1 1.3 fusion.7
  216.9 12.1 %all_to_all.32 = bf16[4,17,3584]{2,1,0:T(8,128)(2,1)} all-to-all(bf16[4,17,3584]{2,1,0:T(8,128)(2,1)S(1)} %reshape.93), channel_id=1, replica_groups=mesh['pp'=16,'x'=4,'y'=8] {'x'}, dimensions={0} | all-to-all | bytes 974848 | tf_op jit(solution)/shard_map/all_to_all | solution.py:28
  229.0 1.3 reshape.94
  230.6 94.7 %all_to_all.33 = bf16[8,72,3584]{2,1,0:T(8,128)(2,1)S(1)} all-to-all(bf16[8,72,3584]{2,1,0:T(8,128)(2,1)S(1)} %stack.12), channel_id=1, replica_groups=mesh['pp'=16,'x'=4,'y'=8] {'y'}, dimensions={0} | all-to-all | bytes 8257536 | tf_op jit(solution)/shard_map/all_to_all | solution.py:34
  325.3 1.9 copy-done.2
  327.2 1.2 fusion.19
  328.5 8.5 %convolution_convert_fusion = bf16[576,3584]{1,0:T(8,128)(2,1)} fusion(bf16[576,3584]{1,0:T(8,128)(2,1)} %bitcast.60, bf16[1,128,3584]{2,1,0:T(8,128)(2,1)S(1)} %copy-done, bf16[1,3584,128]{2,1,0:T(8,128)(2,1)S(1)} %copy-done.4, f32[576,128]{1,0:T(8,128)S(1)} %fusion.19), kind=kOutput, calls=%fused_computation | convolution fusion | flops 1059471360 | bytes 10387456 | tf_op jit(solution)/shard_map/dot_general | solution.py:38
  337.0 64.0 %reduce-scatter.5.cloned.1.call-done = bf16[72,3584]{1,0:T(8,128)(2,1)} async-done(((bf16[576,3584]{1,0:T(8,128)(2,1)}), bf16[72,3584]{1,0:T(8,128)(2,1)}) %reduce-scatter.5.cloned.1.call-update) | async-done | bytes 516112 | tf_op jit(solution)/shard_map/reduce_scatter | solution.py:39
  400.9 1.2 reshape.96
  402.1 15.2 %all_to_all.34 = bf16[4,17,3584]{2,1,0:T(8,128)(2,1)S(1)} all-to-all(bf16[4,17,3584]{2,1,0:T(8,128)(2,1)S(1)} %reshape.96), channel_id=1, replica_groups=mesh['pp'=16,'x'=4,'y'=8] {'x'}, dimensions={0} | all-to-all | bytes 974848 | tf_op jit(solution)/shard_map/all_to_all | solution.py:41
  417.9 1.0 maximum_bitcast_fusion
  (45 shorter events, 5.2 us)
Async XLA Ops:
  6.5 121.7 %copy-start = (bf16[1,128,3584]{2,1,0:T(8,128)(2,1)S(1)}, bf16[1,128,3584]{2,1,0:T(8,128)(2,1)}, u32[]{:S(2)}) copy-start(bf16[1,128,3584]{2,1,0:T(8,128)(2,1)} %param.13) | copy-start | bytes 2752516
  6.5 187.8 %reduce-scatter.3.cloned.1.call-start = ((), (), s32[]{:S(2)}) async-start(), calls=%async_computation.8 | async-start | bytes 4644864 | tf_op jit(solution)/shard_map/reduce_scatter | solution.py:39
  27.9 99.1 %copy-start.8 = (bf16[1,3584,128]{2,1,0:T(8,128)(2,1)S(1)}, bf16[1,3584,128]{2,1,0:T(8,128)(2,1)}, u32[]{:S(2)}) copy-start(bf16[1,3584,128]{2,1,0:T(8,128)(2,1)} %param.11) | copy-start | bytes 2752516
  125.0 1.9 copy-start.1
  125.0 3.2 copy-start.4
  136.7 63.9 %copy-start.7 = (f32[2,1,64,1]{2,3,1,0:T(1,128)S(1)}, f32[2,1,64,1]{2,3,1,0:T(1,128)}, u32[]{:S(2)}) copy-start(f32[2,1,64,1]{2,3,1,0:T(1,128)} %param.15) | copy-start | bytes 1540
  136.7 75.3 %copy-start.3 = (bf16[1,64,3584]{2,1,0:T(8,128)(2,1)S(1)}, bf16[1,64,3584]{2,1,0:T(8,128)(2,1)}, u32[]{:S(2)}) copy-start(bf16[1,64,3584]{2,1,0:T(8,128)(2,1)} %param.8) | copy-start | bytes 1376260
  196.4 15.4 %all-to-all-start.2 = ((bf16[4,17,3584]{2,1,0:T(8,128)(2,1)}), bf16[4,17,3584]{2,1,0:T(8,128)(2,1)S(1)}, u32[]{:S(2)}, u32[]{:S(2)}) async-start(bf16[4,17,3584]{2,1,0:T(8,128)(2,1)} %reshape.91), calls=%async_computation.3 | async-start | bytes 1376256 | tf_op jit(solution)/shard_map/all_to_all | solution.py:41
  200.6 200.3 %reduce-scatter.5.cloned.1.call-start = ((), (), s32[]{:S(2)}) async-start(), calls=%async_computation.9 | async-start | bytes 4644864 | tf_op jit(solution)/shard_map/reduce_scatter | solution.py:39
  212.3 4.0 copy-start.5
  212.4 2.7 collective-permute-start
  230.6 96.7 %copy-start.9 = (bf16[1,3584,128]{2,1,0:T(8,128)(2,1)S(1)}, bf16[1,3584,128]{2,1,0:T(8,128)(2,1)}, u32[]{:S(2)}) copy-start(bf16[1,3584,128]{2,1,0:T(8,128)(2,1)} %param.11) | copy-start | bytes 2752516
  325.3 1.9 copy-start.2
  337.0 80.9 %copy-start.6 = (bf16[64,3584]{1,0:T(8,128)(2,1)S(1)}, bf16[64,3584]{1,0:T(8,128)(2,1)}, u32[]{:S(2)}) copy-start(bf16[64,3584]{1,0:T(8,128)(2,1)} %copy-done.5) | copy-start | bytes 1376260
Sparse Core Ops, SparseCore 0:
  136.8 57.4 reduce-scatter.2
  337.1 63.7 reduce-scatter.4
